TPU v7x, 256 devices: a whole 4x4x8 slice. The times are simulated.
256 devices in a mesh: dp: 8 (over z), seq: 32 (over x, y, core).
Axes of the slice: x: 4, y: 4, z: 8, core: 2. Of those that a mesh axis runs over, the one named last changes fastest.
Arguments:
- latents: bfloat16 [128, 2048], P(None, 'seq'), may hold values from -6 to 6
- saved_keys: bfloat16 [8, 24576, 2048], P('dp', 'seq'), may hold values from -6 to 6
- saved_values: bfloat16 [8, 24576, 2048], P('dp', 'seq'), may hold values from -6 to 6
- out_grad: bfloat16 [8, 128, 2048], P('dp', None, 'seq'), may hold values from -24576 to 24576, as said below
- out_saved: bfloat16 [8, 128, 2048], P('dp', None, 'seq'), may hold values from -6 to 6
- log_norm: float32 [8, 16, 128], P('dp'), as said below
Outputs:
- latent_grad: float32 [128, 2048], P(None, 'seq')
- key_grad: bfloat16 [8, 24576, 2048], P('dp', 'seq')
- value_grad: bfloat16 [8, 24576, 2048], P('dp', 'seq')
Inputs may be any that keep to these rules, and one draw needn't show every extreme that they name: `log_norm`: each entry lies between the natural logarithm of 24576 minus 0.5 and that logarithm plus 1.5. `out_grad`: entries have magnitudes of order 24576 / 16 and lie within plus or minus 24576.
All inputs are finite; a program needn't handle non-finite values.
Results may differ from a plain program's by a relative error of at most 0.0015.
The roundings to bfloat16 on the way count: a program that leaves them out, or rounds other values in their place, can miss the bound.
Values may be sent and summed in bfloat16 or wider, within the bound.
A program may use at most 64 MiB of HBM per device.

v0:
```python
import jax
import jax.numpy as jnp
from jax import lax
from jax.sharding import PartitionSpec as P

HEADS = 16
HEAD_DIM = 128
LATENTS = 128


def in_order(tiles, dim):
    shape = list(tiles.shape[1:])
    shape[dim] *= tiles.shape[0]
    return jnp.moveaxis(tiles, 0, dim).reshape(shape)


def copy_for_each(shard, axis):
    copies = jnp.broadcast_to(shard, (lax.axis_size(axis), *shard.shape))
    return lax.all_to_all(copies, axis, split_axis=0, concat_axis=0, tiled=True)


def gathered_copies(shard, axis, dim):
    return in_order(copy_for_each(shard, axis), dim)


def side_by_side(arrays, axis, dim, along):
    both = jnp.concatenate(arrays, axis=along)
    result, at, gathered = (gathered_copies(both, axis, dim), 0, [])
    for a in arrays:
        gathered.append(lax.slice_in_dim(result, at, at + a.shape[along], axis=along))
        at += a.shape[along]
    return tuple(gathered)


def split_up(shard, dim, size):
    before, after = (shard.shape[:dim], shard.shape[dim + 1 :])
    return jnp.moveaxis(shard.reshape(*before, size, -1, *after), dim, 0)


def summed_on_arrival(shard, axis, dim):
    size = lax.axis_size(axis)
    tiles = lax.all_to_all(split_up(shard, dim, size), axis, 0, 0, tiled=True)
    return jnp.sum(tiles, axis=0)


def of_everyone(shard, axis):
    return copy_for_each(shard, axis).sum(axis=0)


def local(latents, saved_keys, saved_values, out_grad, out_saved, log_norm):
    score_scale = HEAD_DIM ** (-0.5)
    token_count = saved_keys.shape[1]
    queries, grad_rows, saved_rows = side_by_side((latents, out_grad[0], out_saved[0]), "seq", 1, 0)
    products = grad_rows.astype(jnp.float32) * saved_rows.astype(jnp.float32)
    row_dots = jnp.sum(products.reshape(LATENTS, HEADS, HEAD_DIM), axis=2).T
    query_heads = queries.reshape(LATENTS, HEADS, HEAD_DIM)
    grad_heads = grad_rows.reshape(LATENTS, HEADS, HEAD_DIM)
    key_heads = saved_keys[0].reshape(token_count, HEADS, HEAD_DIM)
    value_heads = saved_values[0].reshape(token_count, HEADS, HEAD_DIM)
    scores = (
        jnp.einsum("lhc,thc->hlt", query_heads, key_heads, preferred_element_type=jnp.float32)
        * score_scale
    )
    weights = jnp.exp(scores - log_norm[0][:, :, None])
    weights_low = weights.astype(jnp.bfloat16)
    value_grad = jnp.einsum(
        "hlt,lhc->thc", weights_low, grad_heads, preferred_element_type=jnp.float32
    )
    weight_grad = jnp.einsum(
        "lhc,thc->hlt", grad_heads, value_heads, preferred_element_type=jnp.float32
    )
    score_low = (score_scale * weights * (weight_grad - row_dots[:, :, None])).astype(jnp.bfloat16)
    key_grad = jnp.einsum(
        "hlt,lhc->thc", score_low, query_heads, preferred_element_type=jnp.float32
    )
    query_part = jnp.einsum(
        "hlt,thc->lhc", score_low, key_heads, preferred_element_type=jnp.float32
    ).reshape(LATENTS, HEADS * HEAD_DIM)
    share_part = summed_on_arrival(query_part, "seq", 1)
    latent_grad = of_everyone(share_part, "dp")
    key_out = key_grad.reshape(1, token_count, HEADS * HEAD_DIM).astype(jnp.bfloat16)
    value_out = value_grad.reshape(1, token_count, HEADS * HEAD_DIM).astype(jnp.bfloat16)
    return (latent_grad, key_out, value_out)


def solution(mesh):
    placed = (
        P(None, "seq"),
        P("dp", "seq", None),
        P("dp", "seq", None),
        P("dp", None, "seq"),
        P("dp", None, "seq"),
        P("dp", None, None),
    )
    return jax.shard_map(
        local,
        mesh=mesh,
        in_specs=placed,
        out_specs=(P(None, "seq"), P("dp", "seq", None), P("dp", "seq", None)),
        check_vma=False,
    )
```

profile of v0, /device:TPU:1, one launch (start us, length us, event | category | flops | bytes accessed | tf_op | source)
XLA Modules:
  0.0 90.3 jit_solution(9139352244409815220)
XLA Ops:
  0.6 0.8 pad_maximum_fusion
  1.4 1.4 %broadcast_in_dim.7 = bf16[32,384,64]{1,2,0:T(8,128)(2,1)} broadcast(bf16[384,64]{0,1:T(8,128)(2,1)S(1)} %pad_maximum_fusion), dimensions={1,2} | broadcast | bytes 1622016 | tf_op jit(solution)/shard_map/broadcast_in_dim | solution.py:18
  2.8 8.6 %all-to-all-start = ((bf16[32,384,64]{1,2,0:T(8,128)(2,1)}), bf16[32,384,64]{1,2,0:T(8,128)(2,1)}, u32[]{:S(2)}, u32[]{:S(2)}) async-start(bf16[32,384,64]{1,2,0:T(8,128)(2,1)} %broadcast_in_dim.7), calls=%async_computation | async-start | bytes 3145728 | tf_op jit(solution)/shard_map/all_to_all | solution.py:19
  11.4 3.2 %copy.33 = bf16[1,768,2048]{1,2,0:T(8,128)(2,1)S(1)} copy(bf16[1,768,2048]{2,1,0:T(8,128)(2,1)} %param.7) | data formatting | bytes 6291456 | tf_op jit(solution)/shard_map/reshape;squeeze | solution.py:58
  14.6 4.6 %copy.34 = bf16[96,8,16,128]{3,2,1,0:T(8,128)(2,1)} copy(bf16[96,8,16,128]{3,1,2,0:T(8,128)(2,1)} %bitcast.38) | data formatting | bytes 6291456
  19.2 14.9 %all-to-all-done = bf16[32,384,64]{1,2,0:T(8,128)(2,1)} async-done(((bf16[32,384,64]{1,2,0:T(8,128)(2,1)}), bf16[32,384,64]{1,2,0:T(8,128)(2,1)}, u32[]{:S(2)}, u32[]{:S(2)}) %all-to-all-start) | async-done | bytes 1572896 | tf_op jit(solution)/shard_map/all_to_all | solution.py:19
  34.1 1.4 %multiply_reduce_fusion = f32[128,32]{0,1:T(8,128)S(1)} fusion(bf16[384,32,64]{0,2,1:T(8,128)(2,1)} %bitcast.2), kind=kLoop, calls=%fused_computation.10 | loop fusion | flops 1044480 | bytes 1064960 | tf_op jit(solution)/shard_map/reduce_sum | solution.py:55
  35.5 2.2 %fusion.13 = (bf16[128,32,64]{0,2,1:T(8,128)(2,1)}, bf16[128,32,64]{0,2,1:T(8,128)(2,1)}) fusion(bf16[384,32,64]{0,2,1:T(8,128)(2,1)} %bitcast.2), kind=kLoop, calls=%fused_computation.13 | loop fusion | bytes 2097152 | tf_op jit(solution)/shard_map/slice | solution.py:30
  37.8 0.0 copy-start.2
  37.8 0.0 copy-start.3
  37.8 0.0 copy-start.4
  37.8 2.2 %fusion.14 = f32[16,128,768]{2,1,0:T(8,128)S(1)} fusion(bf16[128,16,128]{0,2,1:T(8,128)(2,1)} %bitcast.35, bf16[768,16,128]{0,2,1:T(8,128)(2,1)S(1)} %bitcast.31), kind=kOutput, calls=%fused_computation.14 | convolution fusion | flops 402653184 | bytes 9961472 | tf_op jit(solution)/shard_map/lhc,thc->hlt/dot_general | solution.py:61
  40.1 0.0 copy-start
  40.1 0.0 copy-done.2
  40.1 0.0 copy-done.3
  40.1 0.0 copy-done.4
  40.1 3.2 %multiply_convert_fusion = bf16[16,128,768]{2,1,0:T(8,128)(2,1)S(1)} fusion(f32[16,128,768]{2,1,0:T(8,128)S(1)} %fusion.14, f32[16,128]{1,0:T(8,128)S(1)} %bitcast.45, f32[16,128]{1,0:T(8,128)S(1)} %bitcast.46, bf16[128,16,128]{0,2,1:T(8,128)(2,1)S(1)} %bitcast.41, bf16[768,16,128]{2,1,0:T(8,128)(2,1)S(1)} %bitcast.39), kind=kOutput, calls=%fused_computation | convolution fusion | flops 412090368 | bytes 13123584 | tf_op jit(solution)/shard_map/lhc,thc->hlt/dot_general | solution.py:69
  43.3 0.0 copy-done
  43.3 0.0 copy-start.1
  43.3 2.0 %fusion.15 = f32[16,128,128]{1,2,0:T(8,128)} fusion(bf16[16,128,768]{2,1,0:T(8,128)(2,1)S(1)} %multiply_convert_fusion, bf16[768,16,128]{0,2,1:T(8,128)(2,1)S(1)} %bitcast.32), kind=kOutput, calls=%fused_computation.15 | convolution fusion | flops 402653184 | bytes 7340032 | tf_op jit(solution)/shard_map/hlt,thc->lhc/dot_general | solution.py:76
  45.3 0.0 copy-done.1
  45.3 4.8 %all-to-all-start.1 = ((f32[32,128,64]{1,2,0:T(8,128)}), f32[32,128,64]{1,2,0:T(8,128)}, u32[]{:S(2)}, u32[]{:S(2)}) async-start(f32[32,128,64]{1,2,0:T(8,128)} %bitcast.37), calls=%async_computation.1 | async-start | bytes 2097152 | tf_op jit(solution)/shard_map/all_to_all | solution.py:42
  50.1 3.0 %convolution_convert_fusion = bf16[16,128,768]{2,1,0:T(8,128)(2,1)S(1)} fusion(bf16[128,16,128]{0,2,1:T(8,128)(2,1)} %bitcast.36, bf16[16,128,768]{2,1,0:T(8,128)(2,1)} %copy-done.1), kind=kOutput, calls=%fused_computation.8 | convolution fusion | flops 404226048 | bytes 6815744 | tf_op jit(solution)/shard_map/hlt,lhc->thc/dot_general | solution.py:73
  53.2 2.9 %copy.29 = bf16[1,768,2048]{2,1,0:T(8,128)(2,1)} copy(bf16[1,768,2048]{1,2,0:T(8,128)(2,1)S(1)} %bitcast.33) | data formatting | bytes 6291456
  56.0 11.2 %all-to-all-done.1 = f32[32,128,64]{1,2,0:T(8,128)} async-done(((f32[32,128,64]{1,2,0:T(8,128)}), f32[32,128,64]{1,2,0:T(8,128)}, u32[]{:S(2)}, u32[]{:S(2)}) %all-to-all-start.1) | async-done | bytes 1048608 | tf_op jit(solution)/shard_map/all_to_all | solution.py:42
  67.2 1.3 %reduce_sum.37 = f32[128,64]{0,1:T(8,128)S(1)} reduce(f32[32,128,64]{1,2,0:T(8,128)} %all-to-all-done.1, f32[]{:T(128)} %constant.1.clone.1), dimensions={0}, to_apply=%region_2.0 | reduce | flops 253952 | bytes 1081348 | tf_op jit(solution)/shard_map/reduce_sum | solution.py:43
  68.5 0.7 broadcast_in_dim.8
  69.2 8.2 %all-to-all-start.2 = ((f32[8,128,64]{1,2,0:T(8,128)}), f32[8,128,64]{1,2,0:T(8,128)S(1)}, u32[]{:S(2)}, u32[]{:S(2)}) async-start(f32[8,128,64]{1,2,0:T(8,128)} %broadcast_in_dim.8), calls=%async_computation.2 | async-start | bytes 524288 | tf_op jit(solution)/shard_map/all_to_all | solution.py:19
  77.4 4.6 %fusion.9 = bf16[16,128,768]{2,1,0:T(8,128)(2,1)S(1)} fusion(bf16[128,16,128]{0,2,1:T(8,128)(2,1)} %bitcast.40, f32[16,128,768]{2,1,0:T(8,128)} %copy-done, f32[16,128]{1,0:T(8,128)S(1)} %bitcast.47), kind=kOutput, calls=%fused_computation.9 | convolution fusion | flops 408944640 | bytes 9969664 | tf_op jit(solution)/shard_map/hlt,lhc->thc/dot_general | solution.py:66
  82.0 2.9 %copy.30 = bf16[1,768,2048]{2,1,0:T(8,128)(2,1)} copy(bf16[1,768,2048]{1,2,0:T(8,128)(2,1)S(1)} %bitcast.34) | data formatting | bytes 6291456
  84.8 4.8 %all-to-all-done.2 = f32[8,128,64]{1,2,0:T(8,128)S(1)} async-done(((f32[8,128,64]{1,2,0:T(8,128)}), f32[8,128,64]{1,2,0:T(8,128)S(1)}, u32[]{:S(2)}, u32[]{:S(2)}) %all-to-all-start.2) | async-done | bytes 262176 | tf_op jit(solution)/shard_map/all_to_all | solution.py:19
  89.7 0.6 reduce_sum.38
  (1 shorter events, 0.0 us)
Async XLA Ops:
  2.8 31.4 %all-to-all-start = ((bf16[32,384,64]{1,2,0:T(8,128)(2,1)}), bf16[32,384,64]{1,2,0:T(8,128)(2,1)}, u32[]{:S(2)}, u32[]{:S(2)}) async-start(bf16[32,384,64]{1,2,0:T(8,128)(2,1)} %broadcast_in_dim.7), calls=%async_computation | async-start | bytes 3145728 | tf_op jit(solution)/shard_map/all_to_all | solution.py:19
  37.8 2.3 %copy-start.2 = (bf16[96,8,16,128]{3,2,1,0:T(8,128)(2,1)S(1)}, bf16[96,8,16,128]{3,2,1,0:T(8,128)(2,1)}, u32[]{:S(2)}) copy-start(bf16[96,8,16,128]{3,2,1,0:T(8,128)(2,1)} %copy.34) | copy-start | bytes 9437188
  37.8 2.3 %copy-start.3 = (bf16[128,32,64]{0,2,1:T(8,128)(2,1)S(1)}, bf16[128,32,64]{0,2,1:T(8,128)(2,1)}, u32[]{:S(2)}) copy-start(bf16[128,32,64]{0,2,1:T(8,128)(2,1)} %get-tuple-element.12) | copy-start | bytes 1572868
  37.8 2.3 %copy-start.4 = (f32[1,16,128]{2,1,0:T(8,128)S(1)}, f32[1,16,128]{2,1,0:T(8,128)}, u32[]{:S(2)}) copy-start(f32[1,16,128]{2,1,0:T(8,128)} %param.11) | copy-start | bytes 24580
  40.1 3.2 %copy-start = (f32[16,128,768]{2,1,0:T(8,128)}, f32[16,128,768]{2,1,0:T(8,128)S(1)}, u32[]{:S(2)}) copy-start(f32[16,128,768]{2,1,0:T(8,128)S(1)} %fusion.14) | copy-start | bytes 18874372
  43.3 2.0 %copy-start.1 = (bf16[16,128,768]{2,1,0:T(8,128)(2,1)}, bf16[16,128,768]{2,1,0:T(8,128)(2,1)S(1)}, u32[]{:S(2)}) copy-start(bf16[16,128,768]{2,1,0:T(8,128)(2,1)S(1)} %multiply_convert_fusion) | copy-start | bytes 9437188
  45.3 21.9 %all-to-all-start.1 = ((f32[32,128,64]{1,2,0:T(8,128)}), f32[32,128,64]{1,2,0:T(8,128)}, u32[]{:S(2)}, u32[]{:S(2)}) async-start(f32[32,128,64]{1,2,0:T(8,128)} %bitcast.37), calls=%async_computation.1 | async-start | bytes 2097152 | tf_op jit(solution)/shard_map/all_to_all | solution.py:42
  69.2 20.5 %all-to-all-start.2 = ((f32[8,128,64]{1,2,0:T(8,128)}), f32[8,128,64]{1,2,0:T(8,128)S(1)}, u32[]{:S(2)}, u32[]{:S(2)}) async-start(f32[8,128,64]{1,2,0:T(8,128)} %broadcast_in_dim.8), calls=%async_computation.2 | async-start | bytes 524288 | tf_op jit(solution)/shard_map/all_to_all | solution.py:19
where the time goes:
time: 91 us; the launch traced here: 90.3 us
  waiting for transfers between devices  31 us (34%)
  starting transfers between devices  21.6 us (24%)
  local copies, waits for them, and re-layouts  17.9 us (20%)
  matrix products  15 us (16%)
  other arithmetic  4.12 us (5%)
    all_to_all x2, waiting for transfers between devices, copy_for_each(): return lax.all_to_all(copies, axis, split_axis=0, concat_axis=0, tiled=True)  19.8 us
    all_to_all x2, starting transfers between devices, copy_for_each(): return lax.all_to_all(copies, axis, split_axis=0, concat_axis=0, tiled=True)  16.8 us
    all_to_all x1, waiting for transfers between devices, summed_on_arrival(): tiles = lax.all_to_all(split_up(shard, dim, size), axis, 0, 0, tiled=True)  11.2 us
    unnamed x13, local copies, waits for them, and re-layouts  10.3 us
    all_to_all x1, starting transfers between devices, summed_on_arrival(): tiles = lax.all_to_all(split_up(shard, dim, size), axis, 0, 0, tiled=True)  4.79 us
    dot_general x1, matrix products, local(): jnp.einsum('hlt,lhc->thc', weights_low, grad_heads, preferred_element_typ...  4.57 us
    dot_general x1, matrix products, local(): jnp.einsum('lhc,thc->hlt', grad_heads, value_heads, preferred_element_typ...  3.19 us
    another operation x1, local copies, waits for them, and re-layouts, local(): key_heads = saved_keys[0].reshape(token_count, HEADS, HEAD_DIM)  3.18 us
  transfers between devices with their start and end apart: 3, of which 3 were waited for; matrix products, arithmetic and copies ran while one was open for 23% of the time, Pallas kernels for 0%

commit v1 on v0

v1 whole, which is shorter than its diff:
```python
import jax
import jax.numpy as jnp
from jax import lax
from jax.experimental import pallas as pl
from jax.experimental.pallas import tpu as pltpu
from jax.sharding import PartitionSpec as P

HEADS = 16
DIM = 128
LATENTS = 128
HALF = DIM // 2
SCALE = DIM ** (-0.5)
LOG2E = 1.4426950408889634
SIDE = 4
CHIPS = SIDE * SIDE
DEPTH = 8
ROWS = 2 * HALF + 16
MESH = pl.DeviceIdType.MESH
BF16 = jnp.bfloat16
F32 = jnp.float32

ORDER = (
    (0, 0), (0, 1), (0, 3), (1, 0), (3, 0), (1, 1), (3, 3), (1, 3),
    (3, 1), (0, 2), (2, 0), (1, 2), (3, 2), (2, 1), (2, 3), (2, 2),
)


def packed_codes(part):
    word = 0
    for at, (dx, dy) in enumerate(part):
        word |= (dx * SIDE + dy) << (4 * at)
    return word - (1 << 32) if word >= 1 << 31 else word


LOW, HIGH = packed_codes(ORDER[:8]), packed_codes(ORDER[8:])


def matmul(a, b, a_dim, b_dim):
    return lax.dot_general(
        a, b, (((a_dim,), (b_dim,)), ((), ())), preferred_element_type=F32
    )


def kernel(
    latents, keys, values, out_grad, out_saved, log_norm,
    share, key_grad, value_grad,
    kb, vb, saved, norms, pack, part, pair_in, pair_sum, reduce_in, z_in,
    local_sem, direct_send, direct_recv, forward_send, forward_recv,
    pair_send, pair_recv, reduce_send, reduce_recv, z_send, z_recv,
):
    z = lax.axis_index("dp")
    seat = lax.axis_index("seq")
    core = seat % 2
    chip = seat // 2
    x, y = chip // SIDE, chip % SIDE
    other = (z, chip * 2 + (1 - core))

    def behind(step):
        word = jnp.where(step < 8, jnp.int32(LOW), jnp.int32(HIGH))
        code = lax.shift_right_logical(word, (step % 8) * 4) % 16
        code = (code + 16) % 16
        return ((x + SIDE - code // SIDE) % SIDE) * SIDE + (y + SIDE - code % SIDE) % SIDE

    def ahead(dx, dy):
        return ((x + dx) % SIDE) * SIDE + (y + dy) % SIDE

    def seat_of(a_chip):
        return (z, a_chip * 2 + core)

    mine = pack.at[chip, core]
    local = [
        pltpu.make_async_copy(latents, mine.at[pl.ds(0, HALF)], local_sem.at[0]),
        pltpu.make_async_copy(out_grad, mine.at[pl.ds(HALF, HALF)], local_sem.at[1]),
        pltpu.make_async_copy(out_saved, saved, local_sem.at[2]),
        pltpu.make_async_copy(log_norm, norms, local_sem.at[3]),
        pltpu.make_async_copy(keys, kb, local_sem.at[4]),
        pltpu.make_async_copy(values, vb, local_sem.at[5]),
    ]
    for copy in local:
        copy.start()

    barrier = pltpu.get_barrier_semaphore()
    for dx, dy in ORDER[1:]:
        pl.semaphore_signal(barrier, inc=1, device_id=seat_of(ahead(dx, dy)), device_id_type=MESH)
    pl.semaphore_signal(barrier, inc=1, device_id=other, device_id_type=MESH)
    for dz in range(1, DEPTH):
        pl.semaphore_signal(barrier, inc=1, device_id=((z + dz) % DEPTH, seat), device_id_type=MESH)

    for copy in local[:3]:
        copy.wait()
    grads = pack[chip, core, HALF : 2 * HALF, :].astype(F32)
    dots = jnp.sum(grads * saved[...].astype(F32), axis=0, keepdims=True)
    top = dots.astype(BF16).astype(F32)
    middle = (dots - top).astype(BF16).astype(F32)
    rest = dots - top - middle
    row = lax.broadcasted_iota(jnp.int32, (16, DIM), 0)
    rows = jnp.where(row == 0, top, jnp.where(row == 1, middle, jnp.where(row == 2, rest, 0.0)))
    pack[chip, core, 2 * HALF : ROWS, :] = rows.astype(BF16)

    pl.semaphore_wait(barrier, CHIPS - 1 + 1 + DEPTH - 1)

    def direct(to):
        return pltpu.make_async_remote_copy(
            src_ref=mine, dst_ref=mine,
            send_sem=direct_send.at[to], recv_sem=direct_recv.at[chip],
            device_id=seat_of(to), device_id_type=MESH,
        )

    def direct_from(head):
        return pltpu.make_async_remote_copy(
            src_ref=mine, dst_ref=pack.at[head, core],
            send_sem=direct_send.at[head], recv_sem=direct_recv.at[head],
            device_id=seat_of(head), device_id_type=MESH,
        )

    def forward(head):
        return pltpu.make_async_remote_copy(
            src_ref=pack.at[head, core], dst_ref=pack.at[head, core],
            send_sem=forward_send.at[head], recv_sem=forward_recv.at[head],
            device_id=other, device_id_type=MESH,
        )

    def forward_from(head):
        return pltpu.make_async_remote_copy(
            src_ref=pack.at[head, core], dst_ref=pack.at[head, 1 - core],
            send_sem=forward_send.at[head], recv_sem=forward_recv.at[head],
            device_id=other, device_id_type=MESH,
        )

    def pair(head):
        return pltpu.make_async_remote_copy(
            src_ref=part.at[head, 1 - core], dst_ref=pair_in.at[head],
            send_sem=pair_send.at[head], recv_sem=pair_recv.at[head],
            device_id=other, device_id_type=MESH,
        )

    def reduce(head):
        return pltpu.make_async_remote_copy(
            src_ref=pair_sum.at[head], dst_ref=reduce_in.at[chip],
            send_sem=reduce_send.at[head], recv_sem=reduce_recv.at[chip],
            device_id=seat_of(head), device_id_type=MESH,
        )

    def reduce_from(head):
        return pltpu.make_async_remote_copy(
            src_ref=pair_sum.at[head], dst_ref=reduce_in.at[head],
            send_sem=reduce_send.at[head], recv_sem=reduce_recv.at[head],
            device_id=seat_of(head), device_id_type=MESH,
        )

    forward(chip).start()
    for dx, dy in ORDER[1:]:
        direct(ahead(dx, dy)).start()
    for copy in local[3:]:
        copy.wait()

    def combine(head):
        pair(head).wait_recv()
        pair_sum[head] = part[head, core] + pair_in[head]

    def meet(step, carry):
        head = behind(step)

        @pl.when(step < CHIPS - 1)
        def _():
            following = behind(step + 1)
            direct_from(following).wait_recv()
            forward(following).start()

        forward_from(head).wait_recv()
        columns = pl.ds(pl.multiple_of(head * DIM, DIM), DIM)
        query = jnp.concatenate([pack[head, 0, :HALF, :], pack[head, 1, :HALF, :]], axis=0)
        grad = jnp.concatenate(
            [pack[head, 0, HALF : 2 * HALF, :], pack[head, 1, HALF : 2 * HALF, :]], axis=0
        )
        dot_rows = pack[head, 0, 2 * HALF : ROWS, :].astype(F32)
        dot_rows += pack[head, 1, 2 * HALF : ROWS, :].astype(F32)
        row_dots = jnp.sum(dot_rows, axis=0, keepdims=True)
        norm = norms[pl.ds(head, 1), :] * LOG2E
        key = kb[:, columns]
        scores = matmul(key, query, 1, 0)
        weight_grad = matmul(vb[:, columns], grad, 1, 0)
        weights = jnp.exp2(scores * (SCALE * LOG2E) - norm)
        score_low = ((SCALE * weights) * (weight_grad - row_dots)).astype(BF16)
        terms = matmul(key, score_low, 0, 0)
        part[head, 0] = terms[:HALF]
        part[head, 1] = terms[HALF:]
        pair(head).start()
        value_grad[:, columns] = matmul(weights.astype(BF16), grad, 1, 1).astype(BF16)
        key_grad[:, columns] = matmul(score_low, query, 1, 1).astype(BF16)

        @pl.when(step >= 1)
        def _():
            before = behind(jnp.maximum(step - 1, 0))
            combine(before)

            @pl.when(step >= 2)
            def _():
                reduce(before).start()

        return carry

    lax.fori_loop(0, CHIPS, meet, 0)
    last = behind(jnp.int32(CHIPS - 1))
    combine(last)
    reduce(last).start()

    total = pair_sum[chip]
    for dx, dy in ORDER[1:]:
        sender = ahead(dx, dy)
        reduce_from(sender).wait_recv()
        total += reduce_in[sender]
    z_in[z] = total

    def cross(to):
        return pltpu.make_async_remote_copy(
            src_ref=z_in.at[z], dst_ref=z_in.at[z],
            send_sem=z_send.at[to], recv_sem=z_recv.at[z],
            device_id=(to, seat), device_id_type=MESH,
        )

    def cross_from(sender):
        return pltpu.make_async_remote_copy(
            src_ref=z_in.at[z], dst_ref=z_in.at[sender],
            send_sem=z_send.at[sender], recv_sem=z_recv.at[sender],
            device_id=(sender, seat), device_id_type=MESH,
        )

    for dz in (4, 3, 5, 2, 6, 1, 7):
        cross((z + dz) % DEPTH).start()
    for dz in (1, 7, 2, 6, 3, 5, 4):
        cross_from((z + dz) % DEPTH).wait_recv()
    result = z_in[0]
    for at in range(1, DEPTH):
        result += z_in[at]
    share[...] = result

    forward(chip).wait_send()
    pair(chip).wait_send()
    for dx, dy in ORDER[1:]:
        to = ahead(dx, dy)
        direct(to).wait_send()
        forward(to).wait_send()
        pair(to).wait_send()
        reduce(to).wait_send()
    for dz in range(1, DEPTH):
        cross((z + dz) % DEPTH).wait_send()


def local(latents, saved_keys, saved_values, out_grad, out_saved, log_norm):
    tokens, width = saved_keys.shape[1:]
    dma = pltpu.SemaphoreType.DMA
    hbm = pl.BlockSpec(memory_space=pltpu.MemorySpace.HBM)
    vmem = pl.BlockSpec(memory_space=pltpu.MemorySpace.VMEM)
    share, key_grad, value_grad = pl.pallas_call(
        kernel,
        name="resampler_backward",
        out_shape=(
            jax.ShapeDtypeStruct((HALF, LATENTS), F32),
            jax.ShapeDtypeStruct((tokens, width), BF16),
            jax.ShapeDtypeStruct((tokens, width), BF16),
        ),
        in_specs=[hbm] * 6,
        out_specs=(vmem, vmem, vmem),
        scratch_shapes=[
            pltpu.VMEM((tokens, width), BF16),
            pltpu.VMEM((tokens, width), BF16),
            pltpu.VMEM((HALF, LATENTS), BF16),
            pltpu.VMEM((HEADS, LATENTS), F32),
            pltpu.VMEM((CHIPS, 2, ROWS, LATENTS), BF16),
            pltpu.VMEM((CHIPS, 2, HALF, LATENTS), F32),
            pltpu.VMEM((CHIPS, HALF, LATENTS), F32),
            pltpu.VMEM((CHIPS, HALF, LATENTS), F32),
            pltpu.VMEM((CHIPS, HALF, LATENTS), F32),
            pltpu.VMEM((DEPTH, HALF, LATENTS), F32),
            dma((6,)),
            dma((CHIPS,)), dma((CHIPS,)), dma((CHIPS,)), dma((CHIPS,)),
            dma((CHIPS,)), dma((CHIPS,)), dma((CHIPS,)), dma((CHIPS,)),
            dma((DEPTH,)), dma((DEPTH,)),
        ],
        compiler_params=pltpu.CompilerParams(
            collective_id=0, has_side_effects=True, vmem_limit_bytes=40 << 20
        ),
    )(
        *(pltpu.with_memory_space_constraint(a, pltpu.MemorySpace.HBM) for a in (latents.T, saved_keys[0], saved_values[0], out_grad[0].T, out_saved[0].T, log_norm[0]))
    )
    return share.T, key_grad[None], value_grad[None]


def solution(mesh):
    placed = (
        P(None, "seq"),
        P("dp", "seq", None),
        P("dp", "seq", None),
        P("dp", None, "seq"),
        P("dp", None, "seq"),
        P("dp", None, None),
    )
    return jax.shard_map(
        local,
        mesh=mesh,
        in_specs=placed,
        out_specs=(P(None, "seq"), P("dp", "seq", None), P("dp", "seq", None)),
        check_vma=False,
    )
```

time: 91 us -> 49.2 us (0.54)
  Pallas kernels: 0 us -> 44.5 us
  waiting for transfers between devices: 31 us -> 0 us
  starting transfers between devices: 21.6 us -> 0 us
  matrix products: 15 us -> 0 us
  local copies, waits for them, and re-layouts: 17.9 us -> 3.94 us
  other arithmetic: 4.12 us -> 0 us
    pallas_call x0 -> x1, Pallas kernels: none -> 44.5 us  [local(): pl.pallas_call(kernel, name='resampler_backward', out_shape=(jax.ShapeDty...]
    all_to_all x3 -> x0, waiting for transfers between devices: 31 us -> none  [the longest x2 19.8 us: copy_for_each(): return lax.all_to_all(copies, axis, split_axis=0, concat_axis=0, tiled=True)]
    all_to_all x3 -> x0, starting transfers between devices: 21.6 us -> none  [the longest x2 16.8 us: copy_for_each(): return lax.all_to_all(copies, axis, split_axis=0, concat_axis=0, tiled=True)]
    dot_general x5 -> x0, matrix products: 15 us -> none  [the longest x1 4.57 us: local(): jnp.einsum('hlt,lhc->thc', weights_low, grad_heads, preferred_element_typ...]
    unnamed x13 -> x3, local copies, waits for them, and re-layouts: 10.3 us -> 3.94 us
    reduce_sum x4 -> x0, other arithmetic: 3.36 us -> none  [the longest x2 1.44 us: local(): row_dots = jnp.sum(products.reshape(LATENTS, HEADS, HEAD_DIM), axis=2).T]
    another operation x1 -> x0, local copies, waits for them, and re-layouts: 3.18 us -> none  [local(): key_heads = saved_keys[0].reshape(token_count, HEADS, HEAD_DIM)]
    slice x1 -> x0, local copies, waits for them, and re-layouts: 2.24 us -> none  [side_by_side(): lax.slice_in_dim(result, at, at + a.shape[along], axis=along)]
  transfers between devices with their start and end apart: 3 -> 0, of which waited for: 3 -> 0; matrix products, arithmetic and copies ran while one was open for 23% -> 0% of each run, Pallas kernels for 0% -> 0%
where the time goes in v1:
time: 49.2 us; the launch traced here: 49.1 us
  Pallas kernels  44.5 us (90%)
  local copies, waits for them, and re-layouts  3.94 us (8%)
  between operations  0.64 us (1%)
    pallas_call x1, Pallas kernels, local(): pl.pallas_call(kernel, name='resampler_backward', out_shape=(jax.ShapeDty...  44.5 us
    unnamed x3, local copies, waits for them, and re-layouts  3.94 us

profile of v1, /device:TPU:1, one launch (start us, length us, event | category | flops | bytes accessed | tf_op | source)
XLA Modules:
  0.0 49.1 jit_solution(15792327182423604331)
XLA Ops:
  0.6 44.5 %resampler_backward.1 = (f32[64,128]{1,0:T(8,128)S(1)}, bf16[768,2048]{1,0:T(8,128)(2,1)S(1)}, bf16[768,2048]{1,0:T(8,128)(2,1)S(1)}) custom-call(bf16[64,128]{1,0:T(8,128)(2,1)} %bitcast.18, bf16[768,2048]{1,0:T(8,128)(2,1)} %bitcast.16, bf16[768,2048]{1,0:T(8,128)(2,1)} %bitcast.17, bf16[64,128]{1,0:T(8,128)(2,1)} %bitcast.19, bf16[64,128]{1,0:T(8,128)(2,1)} %bitcast.20, ...), custom_call_target="tpu_custom_call" | custom-call | tf_op jit(solution)/shard_map/resampler_backward/pallas_call | solution.py:255
  45.1 0.6 %copy.12 = f32[128,64]{0,1:T(8,128)} copy(f32[128,64]{0,1:T(8,128)S(1)} %bitcast.15) | data formatting | bytes 65536
  45.7 1.7 %copy.13 = bf16[1,768,2048]{2,1,0:T(8,128)(2,1)} copy(bf16[1,768,2048]{2,1,0:T(8,128)(2,1)S(1)} %bitcast.14) | data formatting | bytes 6291456
  47.4 1.7 %copy.14 = bf16[1,768,2048]{2,1,0:T(8,128)(2,1)} copy(bf16[1,768,2048]{2,1,0:T(8,128)(2,1)S(1)} %bitcast.13) | data formatting | bytes 6291456

commit v2 on v1

v2 whole, which is shorter than its diff:
```python
import jax
import jax.numpy as jnp
from jax import lax
from jax.experimental import pallas as pl
from jax.experimental.pallas import tpu as pltpu
from jax.sharding import PartitionSpec as P

HEADS = 16
DIM = 128
LATENTS = 128
HALF = DIM // 2
SCALE = DIM ** (-0.5)
LOG2E = 1.4426950408889634
SIDE = 4
CHIPS = SIDE * SIDE
DEPTH = 8
ROWS = 2 * HALF + 16
MESH = pl.DeviceIdType.MESH
BF16 = jnp.bfloat16
F32 = jnp.float32

SENDS = (
    (3, 0), (1, 0), (0, 3), (0, 1), (3, 1), (1, 3), (3, 3), (1, 1),
    (2, 0), (0, 2), (2, 3), (2, 1), (3, 2), (1, 2), (2, 2),
)
MEETS = ((0, 0), (0, 1), (1, 0), (3, 0), (1, 1), (3, 1), (2, 0), (2, 1))
WORD = sum((dx + SIDE * row) << (4 * at) for at, (dx, row) in enumerate(MEETS))
STEPS = len(MEETS)
PIECES = 4


def matmul(a, b, a_dim, b_dim):
    return lax.dot_general(
        a, b, (((a_dim,), (b_dim,)), ((), ())), preferred_element_type=F32
    )


def kernel(
    latents, keys, values, out_grad, out_saved, log_norm,
    share, key_grad, value_grad,
    kb, vb, saved, norms, mine, pack, terms, parts, reduce_in, z_in, key_stage, value_stage,
    local_sem, token_sem, token_send, token_recv, pack_send, pack_recv,
    back_send, back_recv, reduce_send, reduce_recv, z_send, z_recv,
):
    z = lax.axis_index("dp")
    seat = lax.axis_index("seq")
    core = seat % 2
    chip = seat // 2
    x, y = chip // SIDE, chip % SIDE
    parity = chip % 2
    other = (z, chip * 2 + (1 - core))

    def head_at(step, of_core):
        code = lax.shift_right_logical(jnp.int32(WORD), jnp.int32(step) * 4) % 8
        row = (y // 2 + code // SIDE) % 2
        return ((x + SIDE - code % SIDE) % SIDE) * SIDE + of_core + 2 * row

    def ahead(dx, dy):
        return ((x + dx) % SIDE) * SIDE + (y + dy) % SIDE

    def columns_of(head):
        return pl.ds(pl.multiple_of(head * DIM, DIM), DIM)

    def tokens_in(step):
        head = head_at(step, core)
        cut = columns_of(head)
        at = head // 2
        return (
            pltpu.make_async_copy(keys.at[:, cut], kb.at[0, at], token_sem.at[0, at]),
            pltpu.make_async_copy(values.at[:, cut], vb.at[0, at], token_sem.at[1, at]),
        )

    def tokens_over(step):
        head = head_at(step, 1 - core)
        cut = columns_of(head)
        at = head // 2
        return tuple(
            pltpu.make_async_remote_copy(
                src_ref=source.at[:, cut], dst_ref=target.at[1, at],
                send_sem=token_send.at[n, at], recv_sem=token_recv.at[n, at],
                device_id=other, device_id_type=MESH,
            )
            for n, (source, target) in enumerate(((keys, kb), (values, vb)))
        )

    small = [
        pltpu.make_async_copy(latents, mine.at[pl.ds(0, HALF)], local_sem.at[0]),
        pltpu.make_async_copy(out_grad, mine.at[pl.ds(HALF, HALF)], local_sem.at[1]),
        pltpu.make_async_copy(out_saved, saved, local_sem.at[2]),
        pltpu.make_async_copy(log_norm, norms, local_sem.at[3]),
    ]
    for copy in small:
        copy.start()

    barrier = pltpu.get_barrier_semaphore()
    for dx in range(SIDE):
        for dy in range(SIDE):
            for flip in range(2):
                if dx or dy or flip:
                    to = (z, ahead(dx, dy) * 2 + (core + flip) % 2)
                    pl.semaphore_signal(barrier, inc=1, device_id=to, device_id_type=MESH)
    for dz in range(1, DEPTH):
        pl.semaphore_signal(barrier, inc=1, device_id=((z + dz) % DEPTH, seat), device_id_type=MESH)

    for step in range(STEPS):
        for copy in tokens_in(step):
            copy.start()

    for copy in small:
        copy.wait()
    grads = mine[HALF : 2 * HALF, :].astype(F32)
    dots = jnp.sum(grads * saved[...].astype(F32), axis=0, keepdims=True)
    top = dots.astype(BF16).astype(F32)
    middle = (dots - top).astype(BF16).astype(F32)
    rest = dots - top - middle
    row = lax.broadcasted_iota(jnp.int32, (16, DIM), 0)
    rows = jnp.where(row == 0, top, jnp.where(row == 1, middle, jnp.where(row == 2, rest, 0.0)))
    mine[2 * HALF : ROWS, :] = rows.astype(BF16)

    pl.semaphore_wait(barrier, 2 * CHIPS - 1 + DEPTH - 1)

    def give(to):
        return pltpu.make_async_remote_copy(
            src_ref=mine, dst_ref=pack.at[chip // 2, core],
            send_sem=pack_send.at[to], recv_sem=pack_recv.at[chip // 2, core],
            device_id=(z, to * 2 + parity), device_id_type=MESH,
        )

    def given(at, half):
        return pltpu.make_async_remote_copy(
            src_ref=mine, dst_ref=pack.at[at, half],
            send_sem=pack_send.at[at], recv_sem=pack_recv.at[at, half],
            device_id=other, device_id_type=MESH,
        )

    @pl.when(parity != core)
    def _():
        give(chip).start()

    for dx, dy in SENDS:
        give(ahead(dx, dy)).start()
    for step in range(STEPS):
        for copy in tokens_over(step):
            copy.start()

    @pl.when(parity == core)
    def _():
        keep = pltpu.make_async_copy(mine, pack.at[chip // 2, core], local_sem.at[4])
        keep.start()
        keep.wait()

    def reduce(head, half):
        at = head // 2
        return pltpu.make_async_remote_copy(
            src_ref=parts.at[at, half], dst_ref=reduce_in.at[chip],
            send_sem=reduce_send.at[at, half], recv_sem=reduce_recv.at[chip],
            device_id=(z, head * 2 + half), device_id_type=MESH,
        )

    def reduced(sender):
        return pltpu.make_async_remote_copy(
            src_ref=parts.at[0, 0], dst_ref=reduce_in.at[sender],
            send_sem=reduce_send.at[0, 0], recv_sem=reduce_recv.at[sender],
            device_id=other, device_id_type=MESH,
        )

    def back(head):
        cut = columns_of(head)
        at = head // 2
        return tuple(
            pltpu.make_async_remote_copy(
                src_ref=source.at[at], dst_ref=target.at[:, cut],
                send_sem=back_send.at[n, at], recv_sem=back_recv.at[n, at],
                device_id=other, device_id_type=MESH,
            )
            for n, (source, target) in enumerate(
                ((key_stage, key_grad), (value_stage, value_grad))
            )
        )

    def meet(step, carry):
        head = head_at(step, core)
        at = head // 2
        for half in range(2):
            @pl.when((head != chip) | (core != half))
            def _():
                given(at, half).wait_recv()

        query = jnp.concatenate([pack[at, 0, :HALF, :], pack[at, 1, :HALF, :]], axis=0)
        grad = jnp.concatenate(
            [pack[at, 0, HALF : 2 * HALF, :], pack[at, 1, HALF : 2 * HALF, :]], axis=0
        )
        dot_rows = pack[at, 0, 2 * HALF : ROWS, :].astype(F32)
        dot_rows += pack[at, 1, 2 * HALF : ROWS, :].astype(F32)
        row_dots = jnp.sum(dot_rows, axis=0, keepdims=True)
        norm = norms[pl.ds(head, 1), :] * LOG2E

        def scored(side):
            key = kb[side, at]
            scores = matmul(key, query, 1, 0)
            weight_grad = matmul(vb[side, at], grad, 1, 0)
            weights = jnp.exp2(scores * (SCALE * LOG2E) - norm)
            score_low = ((SCALE * weights) * (weight_grad - row_dots)).astype(BF16)
            return weights.astype(BF16), score_low, matmul(key, score_low, 0, 0)

        for copy in tokens_in(step):
            copy.wait()
        weights_low, score_low, term = scored(0)
        terms[...] = term
        cut = columns_of(head)
        value_grad[:, cut] = matmul(weights_low, grad, 1, 1).astype(BF16)
        key_grad[:, cut] = matmul(score_low, query, 1, 1).astype(BF16)

        for copy in tokens_over(step):
            copy.wait_recv()
        weights_low, score_low, term = scored(1)
        term += terms[...]
        parts[at, 0] = term[:HALF]
        parts[at, 1] = term[HALF:]
        for half in range(2):
            @pl.when((head != chip) | (core != half))
            def _():
                reduce(head, half).start()

        value_stage[at] = matmul(weights_low, grad, 1, 1).astype(BF16)
        key_stage[at] = matmul(score_low, query, 1, 1).astype(BF16)
        for copy in back(head):
            copy.start()
        return carry

    lax.fori_loop(0, STEPS, meet, 0)

    @pl.when(parity == core)
    def _():
        reduce_in[chip] = parts[chip // 2, core]

    @pl.when(parity != core)
    def _():
        reduced(chip).wait_recv()

    total = reduce_in[chip]
    for dx, dy in SENDS:
        sender = ahead(dx, dy)
        reduced(sender).wait_recv()
        total += reduce_in[sender]
    z_in[z] = total

    def cross(to):
        return pltpu.make_async_remote_copy(
            src_ref=z_in.at[z], dst_ref=z_in.at[z],
            send_sem=z_send.at[to], recv_sem=z_recv.at[z],
            device_id=(to, seat), device_id_type=MESH,
        )

    def crossed(sender):
        return pltpu.make_async_remote_copy(
            src_ref=z_in.at[z], dst_ref=z_in.at[sender],
            send_sem=z_send.at[sender], recv_sem=z_recv.at[sender],
            device_id=(sender, seat), device_id_type=MESH,
        )

    for dz in (4, 3, 5, 2, 6, 1, 7):
        cross((z + dz) % DEPTH).start()

    for step in range(STEPS):
        for copy in tokens_over(step):
            copy.wait_send()
        for copy in back(head_at(step, core)):
            copy.wait_send()
        for copy in back(head_at(step, 1 - core)):
            copy.wait_recv()
        head = head_at(step, core)
        for half in range(2):
            @pl.when((head != chip) | (core != half))
            def _():
                reduce(head, half).wait_send()
    for dx, dy in SENDS:
        give(ahead(dx, dy)).wait_send()

    @pl.when(parity != core)
    def _():
        give(chip).wait_send()

    for dz in (1, 7, 2, 6, 3, 5, 4):
        crossed((z + dz) % DEPTH).wait_recv()
    result = z_in[0]
    for at in range(1, DEPTH):
        result += z_in[at]
    share[...] = result
    for dz in range(1, DEPTH):
        cross((z + dz) % DEPTH).wait_send()


def finish(share, key_grad, value_grad, share_out, key_out, value_out, sem):
    copies = [pltpu.make_async_copy(share, share_out, sem.at[0])]
    rows = key_grad.shape[0] // PIECES
    for n, (source, target) in enumerate(((key_grad, key_out), (value_grad, value_out))):
        for at in range(PIECES):
            piece = pl.ds(at * rows, rows)
            copies.append(
                pltpu.make_async_copy(source.at[piece], target.at[piece], sem.at[1 + n * PIECES + at])
            )
    for copy in copies:
        copy.start()
    for copy in copies:
        copy.wait()


def local(latents, saved_keys, saved_values, out_grad, out_saved, log_norm):
    tokens, width = saved_keys.shape[1:]
    dma = pltpu.SemaphoreType.DMA
    hbm = pl.BlockSpec(memory_space=pltpu.MemorySpace.HBM)
    vmem = pl.BlockSpec(memory_space=pltpu.MemorySpace.VMEM)
    held = [
        pltpu.with_memory_space_constraint(a, pltpu.MemorySpace.HBM)
        for a in (
            latents.T, saved_keys[0], saved_values[0], out_grad[0].T, out_saved[0].T, log_norm[0]
        )
    ]
    share, key_grad, value_grad = pl.pallas_call(
        kernel,
        name="resampler_backward",
        out_shape=(
            jax.ShapeDtypeStruct((HALF, LATENTS), F32),
            jax.ShapeDtypeStruct((tokens, width), BF16),
            jax.ShapeDtypeStruct((tokens, width), BF16),
        ),
        in_specs=[hbm] * 6,
        out_specs=(vmem, vmem, vmem),
        scratch_shapes=[
            pltpu.VMEM((2, STEPS, tokens, DIM), BF16),
            pltpu.VMEM((2, STEPS, tokens, DIM), BF16),
            pltpu.VMEM((HALF, LATENTS), BF16),
            pltpu.VMEM((HEADS, LATENTS), F32),
            pltpu.VMEM((ROWS, LATENTS), BF16),
            pltpu.VMEM((STEPS, 2, ROWS, LATENTS), BF16),
            pltpu.VMEM((DIM, LATENTS), F32),
            pltpu.VMEM((STEPS, 2, HALF, LATENTS), F32),
            pltpu.VMEM((CHIPS, HALF, LATENTS), F32),
            pltpu.VMEM((DEPTH, HALF, LATENTS), F32),
            pltpu.VMEM((STEPS, tokens, DIM), BF16),
            pltpu.VMEM((STEPS, tokens, DIM), BF16),
            dma((5,)),
            dma((2, STEPS)), dma((2, STEPS)), dma((2, STEPS)),
            dma((CHIPS,)), dma((STEPS, 2)),
            dma((2, STEPS)), dma((2, STEPS)),
            dma((STEPS, 2)), dma((CHIPS,)),
            dma((DEPTH,)), dma((DEPTH,)),
        ],
        compiler_params=pltpu.CompilerParams(
            collective_id=0, has_side_effects=True, vmem_limit_bytes=40 << 20
        ),
    )(*held)
    share, key_grad, value_grad = pl.pallas_call(
        finish,
        name="results_out",
        out_shape=(
            jax.ShapeDtypeStruct((HALF, LATENTS), F32),
            jax.ShapeDtypeStruct((tokens, width), BF16),
            jax.ShapeDtypeStruct((tokens, width), BF16),
        ),
        in_specs=[vmem] * 3,
        out_specs=(hbm, hbm, hbm),
        scratch_shapes=[dma((1 + 2 * PIECES,))],
        compiler_params=pltpu.CompilerParams(vmem_limit_bytes=1 << 20),
    )(share, key_grad, value_grad)
    return share.T, key_grad[None], value_grad[None]


def solution(mesh):
    placed = (
        P(None, "seq"),
        P("dp", "seq", None),
        P("dp", "seq", None),
        P("dp", None, "seq"),
        P("dp", None, "seq"),
        P("dp", None, None),
    )
    return jax.shard_map(
        local,
        mesh=mesh,
        in_specs=placed,
        out_specs=(P(None, "seq"), P("dp", "seq", None), P("dp", "seq", None)),
        check_vma=False,
    )
```

time: 49.2 us -> 42.6 us (0.87)
  local copies, waits for them, and re-layouts: 3.94 us -> 0 us
  Pallas kernels: 44.5 us -> 41.8 us
    pallas_call x1, Pallas kernels: 44.5 us -> 39 us  [local(): pl.pallas_call(kernel, name='resampler_backward', out_shape=(jax.ShapeDty...]
    unnamed x3 -> x0, local copies, waits for them, and re-layouts: 3.94 us -> none
    pallas_call x0 -> x1, Pallas kernels: none -> 2.76 us  [local(): pl.pallas_call(finish, name='results_out', out_shape=(jax.ShapeDtypeStruc...]
where the time goes in v2:
time: 42.6 us; the launch traced here: 42.4 us
  Pallas kernels  41.8 us (98%)
  between operations  0.64 us (2%)
    pallas_call x1, Pallas kernels, local(): pl.pallas_call(kernel, name='resampler_backward', out_shape=(jax.ShapeDty...  39 us
    pallas_call x1, Pallas kernels, local(): pl.pallas_call(finish, name='results_out', out_shape=(jax.ShapeDtypeStruc...  2.76 us

profile of v2, /device:TPU:1, one launch (start us, length us, event | category | flops | bytes accessed | tf_op | source)
XLA Modules:
  0.0 42.4 jit_solution(15929554660045991306)
XLA Ops:
  0.6 39.0 %resampler_backward.1 = (f32[64,128]{1,0:T(8,128)S(1)}, bf16[768,2048]{1,0:T(8,128)(2,1)S(1)}, bf16[768,2048]{1,0:T(8,128)(2,1)S(1)}) custom-call(bf16[64,128]{1,0:T(8,128)(2,1)} %bitcast.15, bf16[768,2048]{1,0:T(8,128)(2,1)} %bitcast.13, bf16[768,2048]{1,0:T(8,128)(2,1)} %bitcast.14, bf16[64,128]{1,0:T(8,128)(2,1)} %bitcast.16, bf16[64,128]{1,0:T(8,128)(2,1)} %bitcast.17, ...), custom_call_target="tpu_custom_call" | custom-call | tf_op jit(solution)/shard_map/resampler_backward/pallas_call | solution.py:320
  39.6 2.8 %results_out.1 = (f32[64,128]{1,0:T(8,128)}, bf16[768,2048]{1,0:T(8,128)(2,1)}, bf16[768,2048]{1,0:T(8,128)(2,1)}) custom-call(f32[64,128]{1,0:T(8,128)S(1)} %get-tuple-element.9.share, bf16[768,2048]{1,0:T(8,128)(2,1)S(1)} %get-tuple-element.10.key_grad, bf16[768,2048]{1,0:T(8,128)(2,1)S(1)} %get-tuple-element.11.value_grad), custom_call_target="tpu_custom_call" | custom-call | tf_op jit(solution)/shard_map/results_out/pallas_call | solution.py:354

commit v3 on v2

--- a/solution.py
+++ b/solution.py
@@ -14,7 +14,7 @@
 SIDE = 4
 CHIPS = SIDE * SIDE
 DEPTH = 8
-ROWS = 2 * HALF + 16
+ROWS = 2 * HALF + 8
 MESH = pl.DeviceIdType.MESH
 BF16 = jnp.bfloat16
 F32 = jnp.float32
@@ -27,12 +27,45 @@
 WORD = sum((dx + SIDE * row) << (4 * at) for at, (dx, row) in enumerate(MEETS))
 STEPS = len(MEETS)
 PIECES = 4
+BASE, DIGITS = 16, 2
+CODED = HALF + HALF // DIGITS
 
 
 def matmul(a, b, a_dim, b_dim):
     return lax.dot_general(
         a, b, (((a_dim,), (b_dim,)), ((), ())), preferred_element_type=F32
     )
+
+
+def coded(a):
+    high = a.astype(BF16)
+    near = high.astype(F32)
+    over = jnp.where(near == 0.0, 1.0, near)
+    digit = jnp.floor(((a - near) / over) * (128.0 * BASE) + 0.5 * BASE)
+    digit = jnp.clip(digit, 0.0, BASE - 1.0)
+    step = HALF // DIGITS
+    low = digit[:step]
+    for at in range(step, HALF, step):
+        low = low * BASE + digit[at : at + step]
+    return high, (low - 128.0).astype(BF16)
+
+
+def decoded(ref):
+    near = ref[:HALF, :].astype(F32)
+    low = ref[HALF:CODED, :].astype(F32) + 128.0
+    digits = []
+    for _ in range(DIGITS - 1):
+        rest = jnp.floor(low * (1.0 / BASE))
+        digits.append(low - rest * BASE)
+        low = rest
+    digit = jnp.concatenate([low] + digits[::-1], axis=0)
+    return near + near * ((digit + (0.5 - 0.5 * BASE)) * (1.0 / (128.0 * BASE)))
+
+
+def store_coded(ref, a):
+    high, low = coded(a)
+    ref[:HALF, :] = high
+    ref[HALF:CODED, :] = low
 
 
 def kernel(
@@ -113,7 +146,7 @@
     top = dots.astype(BF16).astype(F32)
     middle = (dots - top).astype(BF16).astype(F32)
     rest = dots - top - middle
-    row = lax.broadcasted_iota(jnp.int32, (16, DIM), 0)
+    row = lax.broadcasted_iota(jnp.int32, (8, DIM), 0)
     rows = jnp.where(row == 0, top, jnp.where(row == 1, middle, jnp.where(row == 2, rest, 0.0)))
     mine[2 * HALF : ROWS, :] = rows.astype(BF16)
 
@@ -215,8 +248,8 @@
             copy.wait_recv()
         weights_low, score_low, term = scored(1)
         term += terms[...]
-        parts[at, 0] = term[:HALF]
-        parts[at, 1] = term[HALF:]
+        store_coded(parts.at[at, 0], term[:HALF])
+        store_coded(parts.at[at, 1], term[HALF:])
         for half in range(2):
             @pl.when((head != chip) | (core != half))
             def _():
@@ -238,12 +271,12 @@
     def _():
         reduced(chip).wait_recv()
 
-    total = reduce_in[chip]
+    total = decoded(reduce_in.at[chip])
     for dx, dy in SENDS:
         sender = ahead(dx, dy)
         reduced(sender).wait_recv()
-        total += reduce_in[sender]
-    z_in[z] = total
+        total += decoded(reduce_in.at[sender])
+    store_coded(z_in.at[z], total)
 
     def cross(to):
         return pltpu.make_async_remote_copy(
@@ -283,9 +316,9 @@
 
     for dz in (1, 7, 2, 6, 3, 5, 4):
         crossed((z + dz) % DEPTH).wait_recv()
-    result = z_in[0]
+    result = decoded(z_in.at[0])
     for at in range(1, DEPTH):
-        result += z_in[at]
+        result += decoded(z_in.at[at])
     share[...] = result
     for dz in range(1, DEPTH):
         cross((z + dz) % DEPTH).wait_send()
@@ -335,9 +368,9 @@
             pltpu.VMEM((ROWS, LATENTS), BF16),
             pltpu.VMEM((STEPS, 2, ROWS, LATENTS), BF16),
             pltpu.VMEM((DIM, LATENTS), F32),
-            pltpu.VMEM((STEPS, 2, HALF, LATENTS), F32),
-            pltpu.VMEM((CHIPS, HALF, LATENTS), F32),
-            pltpu.VMEM((DEPTH, HALF, LATENTS), F32),
+            pltpu.VMEM((STEPS, 2, CODED, LATENTS), BF16),
+            pltpu.VMEM((CHIPS, CODED, LATENTS), BF16),
+            pltpu.VMEM((DEPTH, CODED, LATENTS), BF16),
             pltpu.VMEM((STEPS, tokens, DIM), BF16),
             pltpu.VMEM((STEPS, tokens, DIM), BF16),
             dma((5,)),

time: 42.6 us -> 40 us (0.939)
  Pallas kernels: 41.8 us -> 39 us
    pallas_call x1, Pallas kernels: 39 us -> 36.2 us  [local(): pl.pallas_call(kernel, name='resampler_backward', out_shape=(jax.ShapeDty...]
where the time goes in v3:
time: 40 us; the launch traced here: 39.6 us
  Pallas kernels  39 us (98%)
  between operations  0.64 us (2%)
    pallas_call x1, Pallas kernels, local(): pl.pallas_call(kernel, name='resampler_backward', out_shape=(jax.ShapeDty...  36.2 us
    pallas_call x1, Pallas kernels, local(): pl.pallas_call(finish, name='results_out', out_shape=(jax.ShapeDtypeStruc...  2.76 us

profile of v3, /device:TPU:1, one launch (start us, length us, event | category | flops | bytes accessed | tf_op | source)
XLA Modules:
  0.0 39.6 jit_solution(11901281133099954989)
XLA Ops:
  0.6 36.2 %resampler_backward.1 = (f32[64,128]{1,0:T(8,128)S(1)}, bf16[768,2048]{1,0:T(8,128)(2,1)S(1)}, bf16[768,2048]{1,0:T(8,128)(2,1)S(1)}) custom-call(bf16[64,128]{1,0:T(8,128)(2,1)} %bitcast.15, bf16[768,2048]{1,0:T(8,128)(2,1)} %bitcast.13, bf16[768,2048]{1,0:T(8,128)(2,1)} %bitcast.14, bf16[64,128]{1,0:T(8,128)(2,1)} %bitcast.16, bf16[64,128]{1,0:T(8,128)(2,1)} %bitcast.17, ...), custom_call_target="tpu_custom_call" | custom-call | tf_op jit(solution)/shard_map/resampler_backward/pallas_call | solution.py:353
  36.8 2.8 %results_out.1 = (f32[64,128]{1,0:T(8,128)}, bf16[768,2048]{1,0:T(8,128)(2,1)}, bf16[768,2048]{1,0:T(8,128)(2,1)}) custom-call(f32[64,128]{1,0:T(8,128)S(1)} %get-tuple-element.9.share, bf16[768,2048]{1,0:T(8,128)(2,1)S(1)} %get-tuple-element.10.key_grad, bf16[768,2048]{1,0:T(8,128)(2,1)S(1)} %get-tuple-element.11.value_grad), custom_call_target="tpu_custom_call" | custom-call | tf_op jit(solution)/shard_map/results_out/pallas_call | solution.py:387

commit v4 on v3

--- a/solution.py
+++ b/solution.py
@@ -27,7 +27,8 @@
 WORD = sum((dx + SIDE * row) << (4 * at) for at, (dx, row) in enumerate(MEETS))
 STEPS = len(MEETS)
 PIECES = 4
-BASE, DIGITS = 16, 2
+EARLY = 6
+BASE, DIGITS = 4, 4
 CODED = HALF + HALF // DIGITS
 
 
@@ -71,7 +72,7 @@
 def kernel(
     latents, keys, values, out_grad, out_saved, log_norm,
     share, key_grad, value_grad,
-    kb, vb, saved, norms, mine, pack, terms, parts, reduce_in, z_in, key_stage, value_stage,
+    kb, vb, saved, norms, mine, pack, terms, parts, reduce_in, z_in, key_stage, value_stage, weights_held, score_held,
     local_sem, token_sem, token_send, token_recv, pack_send, pack_recv,
     back_send, back_recv, reduce_send, reduce_recv, z_send, z_recv,
 ):
@@ -211,6 +212,13 @@
             )
         )
 
+    def both_halves(at):
+        query = jnp.concatenate([pack[at, 0, :HALF, :], pack[at, 1, :HALF, :]], axis=0)
+        grad = jnp.concatenate(
+            [pack[at, 0, HALF : 2 * HALF, :], pack[at, 1, HALF : 2 * HALF, :]], axis=0
+        )
+        return query, grad
+
     def meet(step, carry):
         head = head_at(step, core)
         at = head // 2
@@ -219,10 +227,7 @@
             def _():
                 given(at, half).wait_recv()
 
-        query = jnp.concatenate([pack[at, 0, :HALF, :], pack[at, 1, :HALF, :]], axis=0)
-        grad = jnp.concatenate(
-            [pack[at, 0, HALF : 2 * HALF, :], pack[at, 1, HALF : 2 * HALF, :]], axis=0
-        )
+        query, grad = both_halves(at)
         dot_rows = pack[at, 0, 2 * HALF : ROWS, :].astype(F32)
         dot_rows += pack[at, 1, 2 * HALF : ROWS, :].astype(F32)
         row_dots = jnp.sum(dot_rows, axis=0, keepdims=True)
@@ -240,9 +245,8 @@
             copy.wait()
         weights_low, score_low, term = scored(0)
         terms[...] = term
-        cut = columns_of(head)
-        value_grad[:, cut] = matmul(weights_low, grad, 1, 1).astype(BF16)
-        key_grad[:, cut] = matmul(score_low, query, 1, 1).astype(BF16)
+        weights_held[0, at] = weights_low
+        score_held[0, at] = score_low
 
         for copy in tokens_over(step):
             copy.wait_recv()
@@ -255,13 +259,25 @@
             def _():
                 reduce(head, half).start()
 
-        value_stage[at] = matmul(weights_low, grad, 1, 1).astype(BF16)
-        key_stage[at] = matmul(score_low, query, 1, 1).astype(BF16)
+        weights_held[1, at] = weights_low
+        score_held[1, at] = score_low
+        return carry
+
+    def spread(step, carry):
+        head = head_at(step, core)
+        at = head // 2
+        query, grad = both_halves(at)
+        value_stage[at] = matmul(weights_held[1, at], grad, 1, 1).astype(BF16)
+        key_stage[at] = matmul(score_held[1, at], query, 1, 1).astype(BF16)
         for copy in back(head):
             copy.start()
+        cut = columns_of(head)
+        value_grad[:, cut] = matmul(weights_held[0, at], grad, 1, 1).astype(BF16)
+        key_grad[:, cut] = matmul(score_held[0, at], query, 1, 1).astype(BF16)
         return carry
 
     lax.fori_loop(0, STEPS, meet, 0)
+    lax.fori_loop(0, EARLY, spread, 0)
 
     @pl.when(parity == core)
     def _():
@@ -294,6 +310,7 @@
 
     for dz in (4, 3, 5, 2, 6, 1, 7):
         cross((z + dz) % DEPTH).start()
+    lax.fori_loop(EARLY, STEPS, spread, 0)
 
     for step in range(STEPS):
         for copy in tokens_over(step):
@@ -373,6 +390,8 @@
             pltpu.VMEM((DEPTH, CODED, LATENTS), BF16),
             pltpu.VMEM((STEPS, tokens, DIM), BF16),
             pltpu.VMEM((STEPS, tokens, DIM), BF16),
+            pltpu.VMEM((2, STEPS, tokens, DIM), BF16),
+            pltpu.VMEM((2, STEPS, tokens, DIM), BF16),
             dma((5,)),
             dma((2, STEPS)), dma((2, STEPS)), dma((2, STEPS)),
             dma((CHIPS,)), dma((STEPS, 2)),

time: 40 us -> 38.2 us (0.955)
  the two profiles are of different devices: /device:TPU:1 before, /device:TPU:4 now
where the time goes in v4:
time: 38.2 us; the launch traced here: 38.1 us
  Pallas kernels  37.4 us (98%)
  between operations  0.64 us (2%)
    pallas_call x1, Pallas kernels, local(): pl.pallas_call(kernel, name='resampler_backward', out_shape=(jax.ShapeDty...  34.7 us
    pallas_call x1, Pallas kernels, local(): pl.pallas_call(finish, name='results_out', out_shape=(jax.ShapeDtypeStruc...  2.76 us

profile of v4, /device:TPU:4, one launch (start us, length us, event | category | flops | bytes accessed | tf_op | source)
XLA Modules:
  0.0 38.1 jit_solution(5543459962322850943)
XLA Ops:
  0.6 34.7 %resampler_backward.1 = (f32[64,128]{1,0:T(8,128)S(1)}, bf16[768,2048]{1,0:T(8,128)(2,1)S(1)}, bf16[768,2048]{1,0:T(8,128)(2,1)S(1)}) custom-call(bf16[64,128]{1,0:T(8,128)(2,1)} %bitcast.15, bf16[768,2048]{1,0:T(8,128)(2,1)} %bitcast.13, bf16[768,2048]{1,0:T(8,128)(2,1)} %bitcast.14, bf16[64,128]{1,0:T(8,128)(2,1)} %bitcast.16, bf16[64,128]{1,0:T(8,128)(2,1)} %bitcast.17, ...), custom_call_target="tpu_custom_call" | custom-call | tf_op jit(solution)/shard_map/resampler_backward/pallas_call | solution.py:370
  35.3 2.8 %results_out.1 = (f32[64,128]{1,0:T(8,128)}, bf16[768,2048]{1,0:T(8,128)(2,1)}, bf16[768,2048]{1,0:T(8,128)(2,1)}) custom-call(f32[64,128]{1,0:T(8,128)S(1)} %get-tuple-element.9.share, bf16[768,2048]{1,0:T(8,128)(2,1)S(1)} %get-tuple-element.10.key_grad, bf16[768,2048]{1,0:T(8,128)(2,1)S(1)} %get-tuple-element.11.value_grad), custom_call_target="tpu_custom_call" | custom-call | tf_op jit(solution)/shard_map/results_out/pallas_call | solution.py:406

commit v5 on v4

--- a/solution.py
+++ b/solution.py
@@ -23,10 +23,10 @@
     (3, 0), (1, 0), (0, 3), (0, 1), (3, 1), (1, 3), (3, 3), (1, 1),
     (2, 0), (0, 2), (2, 3), (2, 1), (3, 2), (1, 2), (2, 2),
 )
-MEETS = ((0, 0), (0, 1), (1, 0), (3, 0), (1, 1), (3, 1), (2, 0), (2, 1))
+MEETS = ((0, 0), (0, 1), (1, 0), (1, 1), (3, 1), (2, 0), (2, 1), (3, 0))
 WORD = sum((dx + SIDE * row) << (4 * at) for at, (dx, row) in enumerate(MEETS))
 STEPS = len(MEETS)
-PIECES = 4
+PIECES = 16
 EARLY = 6
 BASE, DIGITS = 4, 4
 CODED = HALF + HALF // DIGITS
@@ -38,11 +38,15 @@
     )
 
 
+def power(near):
+    size = jnp.maximum(jnp.abs(near), 1e-30)
+    return jnp.exp2(jnp.floor(jnp.log2(size) + 0.002))
+
+
 def coded(a):
     high = a.astype(BF16)
     near = high.astype(F32)
-    over = jnp.where(near == 0.0, 1.0, near)
-    digit = jnp.floor(((a - near) / over) * (128.0 * BASE) + 0.5 * BASE)
+    digit = jnp.floor((a - near) * ((128.0 * BASE) / power(near)) + 0.5 * BASE)
     digit = jnp.clip(digit, 0.0, BASE - 1.0)
     step = HALF // DIGITS
     low = digit[:step]
@@ -60,7 +64,7 @@
         digits.append(low - rest * BASE)
         low = rest
     digit = jnp.concatenate([low] + digits[::-1], axis=0)
-    return near + near * ((digit + (0.5 - 0.5 * BASE)) * (1.0 / (128.0 * BASE)))
+    return near + power(near) * ((digit + (0.5 - 0.5 * BASE)) * (1.0 / (128.0 * BASE)))
 
 
 def store_coded(ref, a):
@@ -123,18 +127,18 @@
         pltpu.make_async_copy(out_saved, saved, local_sem.at[2]),
         pltpu.make_async_copy(log_norm, norms, local_sem.at[3]),
     ]
+    barrier = pltpu.get_barrier_semaphore()
+    for dz in (4, 3, 5):
+        pl.semaphore_signal(barrier, inc=1, device_id=((z + dz) % DEPTH, seat), device_id_type=MESH)
+    for dx, dy in SENDS[::-1]:
+        for flip in range(2):
+            to = (z, ahead(dx, dy) * 2 + (core + flip) % 2)
+            pl.semaphore_signal(barrier, inc=1, device_id=to, device_id_type=MESH)
+    for dz in (2, 6, 1, 7):
+        pl.semaphore_signal(barrier, inc=1, device_id=((z + dz) % DEPTH, seat), device_id_type=MESH)
+    pl.semaphore_signal(barrier, inc=1, device_id=other, device_id_type=MESH)
     for copy in small:
         copy.start()
-
-    barrier = pltpu.get_barrier_semaphore()
-    for dx in range(SIDE):
-        for dy in range(SIDE):
-            for flip in range(2):
-                if dx or dy or flip:
-                    to = (z, ahead(dx, dy) * 2 + (core + flip) % 2)
-                    pl.semaphore_signal(barrier, inc=1, device_id=to, device_id_type=MESH)
-    for dz in range(1, DEPTH):
-        pl.semaphore_signal(barrier, inc=1, device_id=((z + dz) % DEPTH, seat), device_id_type=MESH)
 
     for step in range(STEPS):
         for copy in tokens_in(step):
@@ -343,12 +347,12 @@
 
 def finish(share, key_grad, value_grad, share_out, key_out, value_out, sem):
     copies = [pltpu.make_async_copy(share, share_out, sem.at[0])]
-    rows = key_grad.shape[0] // PIECES
+    width = key_grad.shape[1] // PIECES
     for n, (source, target) in enumerate(((key_grad, key_out), (value_grad, value_out))):
         for at in range(PIECES):
-            piece = pl.ds(at * rows, rows)
+            cut = pl.ds(at * width, width)
             copies.append(
-                pltpu.make_async_copy(source.at[piece], target.at[piece], sem.at[1 + n * PIECES + at])
+                pltpu.make_async_copy(source.at[:, cut], target.at[:, cut], sem.at[1 + n * PIECES + at])
             )
     for copy in copies:
         copy.start()

time: 38.2 us -> 38.3 us (level)
  the two profiles are of different devices: /device:TPU:4 before, /device:TPU:1 now
where the time goes in v5:
time: 38.3 us; the launch traced here: 37.7 us
  Pallas kernels  37 us (97%)
  between operations  0.64 us (2%)
    pallas_call x1, Pallas kernels, local(): pl.pallas_call(kernel, name='resampler_backward', out_shape=(jax.ShapeDty...  34.1 us
    pallas_call x1, Pallas kernels, local(): pl.pallas_call(finish, name='results_out', out_shape=(jax.ShapeDtypeStruc...  2.93 us

profile of v5, /device:TPU:1, one launch (start us, length us, event | category | flops | bytes accessed | tf_op | source)
XLA Modules:
  0.0 37.7 jit_solution(4687971194931333766)
XLA Ops:
  0.6 34.1 %resampler_backward.1 = (f32[64,128]{1,0:T(8,128)S(1)}, bf16[768,2048]{1,0:T(8,128)(2,1)S(1)}, bf16[768,2048]{1,0:T(8,128)(2,1)S(1)}) custom-call(bf16[64,128]{1,0:T(8,128)(2,1)} %bitcast.15, bf16[768,2048]{1,0:T(8,128)(2,1)} %bitcast.13, bf16[768,2048]{1,0:T(8,128)(2,1)} %bitcast.14, bf16[64,128]{1,0:T(8,128)(2,1)} %bitcast.16, bf16[64,128]{1,0:T(8,128)(2,1)} %bitcast.17, ...), custom_call_target="tpu_custom_call" | custom-call | tf_op jit(solution)/shard_map/resampler_backward/pallas_call | solution.py:374
  34.7 2.9 %results_out.1 = (f32[64,128]{1,0:T(8,128)}, bf16[768,2048]{1,0:T(8,128)(2,1)}, bf16[768,2048]{1,0:T(8,128)(2,1)}) custom-call(f32[64,128]{1,0:T(8,128)S(1)} %get-tuple-element.9.share, bf16[768,2048]{1,0:T(8,128)(2,1)S(1)} %get-tuple-element.10.key_grad, bf16[768,2048]{1,0:T(8,128)(2,1)S(1)} %get-tuple-element.11.value_grad), custom_call_target="tpu_custom_call" | custom-call | tf_op jit(solution)/shard_map/results_out/pallas_call | solution.py:410

commit v6 on v5

--- a/solution.py
+++ b/solution.py
@@ -76,7 +76,7 @@
 def kernel(
     latents, keys, values, out_grad, out_saved, log_norm,
     share, key_grad, value_grad,
-    kb, vb, saved, norms, mine, pack, terms, parts, reduce_in, z_in, key_stage, value_stage, weights_held, score_held,
+    kb, vb, saved, norms, mine, pack, terms, parts, reduce_in, z_in, z_full, key_stage, value_stage, weights_held, score_held,
     local_sem, token_sem, token_send, token_recv, pack_send, pack_recv,
     back_send, back_recv, reduce_send, reduce_recv, z_send, z_recv,
 ):
@@ -335,11 +335,14 @@
     def _():
         give(chip).wait_send()
 
+    z_full[z] = decoded(z_in.at[z])
     for dz in (1, 7, 2, 6, 3, 5, 4):
-        crossed((z + dz) % DEPTH).wait_recv()
-    result = decoded(z_in.at[0])
+        sender = (z + dz) % DEPTH
+        crossed(sender).wait_recv()
+        z_full[sender] = decoded(z_in.at[sender])
+    result = z_full[0]
     for at in range(1, DEPTH):
-        result += decoded(z_in.at[at])
+        result += z_full[at]
     share[...] = result
     for dz in range(1, DEPTH):
         cross((z + dz) % DEPTH).wait_send()
@@ -392,6 +395,7 @@
             pltpu.VMEM((STEPS, 2, CODED, LATENTS), BF16),
             pltpu.VMEM((CHIPS, CODED, LATENTS), BF16),
             pltpu.VMEM((DEPTH, CODED, LATENTS), BF16),
+            pltpu.VMEM((DEPTH, HALF, LATENTS), F32),
             pltpu.VMEM((STEPS, tokens, DIM), BF16),
             pltpu.VMEM((STEPS, tokens, DIM), BF16),
             pltpu.VMEM((2, STEPS, tokens, DIM), BF16),

time: 38.3 us -> 38.3 us (level)
  no operation moved by 1% of the time
where the time goes in v6:
time: 38.3 us; the launch traced here: 37.6 us
  Pallas kernels  37 us (97%)
  between operations  0.64 us (2%)
    pallas_call x1, Pallas kernels, local(): pl.pallas_call(kernel, name='resampler_backward', out_shape=(jax.ShapeDty...  34.1 us
    pallas_call x1, Pallas kernels, local(): pl.pallas_call(finish, name='results_out', out_shape=(jax.ShapeDtypeStruc...  2.93 us

profile of v6, /device:TPU:1, one launch (start us, length us, event | category | flops | bytes accessed | tf_op | source)
XLA Modules:
  0.0 37.6 jit_solution(3922030262291371978)
XLA Ops:
  0.6 34.1 %resampler_backward.1 = (f32[64,128]{1,0:T(8,128)S(1)}, bf16[768,2048]{1,0:T(8,128)(2,1)S(1)}, bf16[768,2048]{1,0:T(8,128)(2,1)S(1)}) custom-call(bf16[64,128]{1,0:T(8,128)(2,1)} %bitcast.15, bf16[768,2048]{1,0:T(8,128)(2,1)} %bitcast.13, bf16[768,2048]{1,0:T(8,128)(2,1)} %bitcast.14, bf16[64,128]{1,0:T(8,128)(2,1)} %bitcast.16, bf16[64,128]{1,0:T(8,128)(2,1)} %bitcast.17, ...), custom_call_target="tpu_custom_call" | custom-call | tf_op jit(solution)/shard_map/resampler_backward/pallas_call | solution.py:377
  34.7 2.9 %results_out.1 = (f32[64,128]{1,0:T(8,128)}, bf16[768,2048]{1,0:T(8,128)(2,1)}, bf16[768,2048]{1,0:T(8,128)(2,1)}) custom-call(f32[64,128]{1,0:T(8,128)S(1)} %get-tuple-element.9.share, bf16[768,2048]{1,0:T(8,128)(2,1)S(1)} %get-tuple-element.10.key_grad, bf16[768,2048]{1,0:T(8,128)(2,1)S(1)} %get-tuple-element.11.value_grad), custom_call_target="tpu_custom_call" | custom-call | tf_op jit(solution)/shard_map/results_out/pallas_call | solution.py:414
